TPU v7x, 32 devices: a whole 2x2x4 slice. The times are simulated.
32 devices in a mesh: seq: 8 (over y, x, core), layer: 4 (over z).
Axes of the slice: x: 2, y: 2, z: 4, core: 2. Of those that a mesh axis runs over, the one named last changes fastest.
Arguments:
- target_enc: bfloat16 [1024, 4096], P('seq'), may hold values from -1000 to 1000
- source_enc: bfloat16 [4, 1024, 4096], P('layer', 'seq'), may hold values from -1000 to 1000
- span_start: int32 [64], replicated, may hold values from 0 to 1015, as said below
- span_end: int32 [64], replicated, may hold values from 8 to 1024, as said below
- span_source: int32 [64], replicated, may hold values from 0 to 3
- norm_gain: float32 [4096], replicated, may hold values from 0.1 to 1.9
- w_key: bfloat16 [4, 4096, 2048], P('layer', None, 'seq'), may hold values from -0.09375 to 0.09375
- w_value: bfloat16 [4, 4096, 2048], P('layer', None, 'seq'), may hold values from -0.09375 to 0.09375
- queries: bfloat16 [4, 512, 2048], P('layer', None, 'seq'), may hold values from -14 to 14
- key_len: int32 [512], replicated, may hold values from 256 to 1024, as said below
Outputs:
- context: bfloat16 [4, 512, 2048], P('layer', None, 'seq')
Inputs may be any that keep to these rules, and one draw needn't show every extreme that they name: `span_start`: span k lies inside the k-th of 64 equal segments of the tokens, starts in the first half of it and covers at least half of it; spans are disjoint and ordered. span_end[k] - span_start[k] is at least half a segment, and span_end[k] is at most the end of the k-th segment. `key_len`: some query token sees all 1024 encoder tokens.
All inputs are finite; a program needn't handle non-finite values.
Results may differ from a plain program's by a relative error of at most 0.003.
The roundings to bfloat16 on the way count: a program that leaves them out, or rounds other values in their place, can miss the bound.
Values may be sent and summed in bfloat16 or wider, within the bound.
A program may use at most 64 MiB of HBM per device.

v0:
```python
import jax
import jax.numpy as jnp
from jax import lax
from jax.sharding import PartitionSpec as P

HEAD = 256


def attend(query, keys, values, keymask, heads_here):
    rows = query.shape[0]
    total = keys.shape[0]
    qheads = query.reshape(rows, heads_here, HEAD)
    kheads = keys.reshape(total, heads_here, HEAD)
    vheads = values.reshape(total, heads_here, HEAD)
    scores = jnp.einsum("qhe,khe->hqk", qheads, kheads, preferred_element_type=jnp.float32)
    scores = jnp.where(keymask[None], scores, -1e30)
    top = jnp.max(scores, axis=-1, keepdims=True)
    expo = jnp.exp(scores - top)
    probs = (expo / jnp.sum(expo, axis=-1, keepdims=True)).astype(jnp.bfloat16)
    mixed = jnp.einsum("hqk,khe->qhe", probs, vheads, preferred_element_type=jnp.float32)
    return mixed.astype(jnp.bfloat16).reshape(rows, heads_here * HEAD)


def per_device(
    target_enc,
    source_enc,
    span_start,
    span_end,
    span_source,
    norm_gain,
    w_key,
    w_value,
    queries,
    key_len,
):
    rows = target_enc.shape[0]
    first_row = lax.axis_index("seq") * rows
    pos = first_row + jnp.arange(rows, dtype=jnp.int32)
    covered = (pos[None, :] >= span_start[:, None]) & (pos[None, :] < span_end[:, None])
    local_runs = source_enc.shape[0]
    run_ids = lax.axis_index("layer") * local_runs + jnp.arange(local_runs, dtype=jnp.int32)
    owner = (span_source[:, None] == run_ids[None, :]).astype(jnp.float32)
    mine = jnp.dot(covered.astype(jnp.float32).T, owner, preferred_element_type=jnp.float32) > 0.5
    term = jnp.sum(jnp.where(mine.T[:, :, None], source_enc.astype(jnp.float32), 0.0), axis=0)
    summed = lax.psum(term.astype(jnp.bfloat16), "layer").astype(jnp.float32)
    hit = jnp.any(covered, axis=0)
    states = jnp.where(hit[:, None], summed, target_enc.astype(jnp.float32))
    meansq = jnp.mean(states * states, axis=-1, keepdims=True)
    normed = (states * lax.rsqrt(meansq + 1e-06) * norm_gain).astype(jnp.bfloat16)
    width = w_key.shape[2]
    heads_here = width // HEAD
    w_both = jnp.concatenate([w_key, w_value], axis=2)
    out = jnp.einsum(
        "rd,ldc->rlc",
        lax.all_gather(normed, "seq", axis=0, tiled=True),
        w_both,
        preferred_element_type=jnp.float32,
    )
    keyval = out.astype(jnp.bfloat16)
    total = keyval.shape[0]
    keymask = jnp.arange(total, dtype=jnp.int32)[None, :] < key_len[:, None]
    keys = keyval[:, 0, :width]
    values = keyval[:, 0, width:]
    outputs = [attend(queries[0], keys, values, keymask, heads_here)]
    return jnp.stack(outputs, axis=0)


def solution(mesh):
    return jax.shard_map(
        per_device,
        mesh=mesh,
        in_specs=(
            P("seq", None),
            P("layer", "seq", None),
            P(),
            P(),
            P(),
            P(),
            P("layer", None, "seq"),
            P("layer", None, "seq"),
            P("layer", None, "seq"),
            P(),
        ),
        out_specs=P("layer", None, "seq"),
        check_vma=False,
    )
```

profile of v0, /device:TPU:0, one launch (start us, length us, event | category | flops | bytes accessed | tf_op | source)
XLA Modules:
  0.0 139.8 jit_solution(13790734928855875518)
XLA Ops:
  6.5 0.0 copy-start
  6.5 0.0 copy-start.4
  6.5 0.0 copy-start.5
  6.5 0.0 copy-start.1
  6.5 0.0 all-reduce.2.cloned.1.call-start
  6.6 1.0 fusion.7
  7.6 2.5 %fusion.8 = bf16[128,4096]{1,0:T(8,128)(2,1)} fusion(bf16[1,128,4096]{2,1,0:T(8,128)(2,1)} %param.11, pred[128]{0:T(512)(128)(4,1)S(1)} %fusion.7), kind=kLoop, calls=%fused_computation.19 | loop fusion | flops 1572864 | bytes 2097280 | tf_op jit(solution)/shard_map/convert_element_type | solution.py:45
  10.1 0.0 copy-start.3
  10.1 0.0 all-reduce.2.cloned.1.call-update
  10.1 0.0 all-gather.2.cloned.1.call-start
  10.2 0.0 copy-done.4
  10.2 0.0 copy-done.5
  10.2 0.1 fusion.10
  10.3 54.5 %all-reduce.2.cloned.1.call-done = bf16[128,4096]{1,0:T(8,128)(2,1)} async-done(((bf16[128,4096]{1,0:T(8,128)(2,1)}), bf16[128,4096]{1,0:T(8,128)(2,1)}) %all-reduce.2.cloned.1.call-update) | async-done | bytes 1048592 | tf_op jit(solution)/shard_map/psum | solution.py:45
  64.8 0.0 copy-done.1
  64.8 0.0 copy-start.2
  64.8 1.8 %multiply_reduce_fusion = f32[128]{0:T(128)S(1)} fusion(bf16[128,4096]{1,0:T(8,128)(2,1)S(1)} %copy-done.1, bf16[128,4096]{1,0:T(8,128)(2,1)} %all-reduce.2.cloned.1.call-done, pred[128]{0:T(512)(128)(4,1)S(1)} %fusion.10), kind=kLoop, calls=%fused_computation.9 | loop fusion | flops 2621312 | bytes 2097792 | tf_op jit(solution)/shard_map/reduce_sum | solution.py:48
  66.6 0.0 copy-done.3
  66.6 0.0 copy-done.2
  66.7 0.0 copy-start.6
  66.7 1.6 %multiply_convert_fusion = bf16[128,4096]{1,0:T(8,128)(2,1)} fusion(bf16[128,4096]{1,0:T(8,128)(2,1)S(1)} %copy-done.1, bf16[128,4096]{1,0:T(8,128)(2,1)S(1)} %copy-done.2, f32[4096]{0:T(1024)S(1)} %copy-done.3, f32[128]{0:T(128)S(1)} %add_rsqrt_fusion, pred[128]{0:T(512)(128)(4,1)S(1)} %fusion.10), kind=kLoop, calls=%fused_computation.8 | loop fusion | flops 3145728 | bytes 3162752 | tf_op jit(solution)/shard_map/convert_element_type | solution.py:49
  68.3 0.0 all-gather.2.cloned.1.call-update
  68.3 0.0 copy-start.7
  68.3 53.9 %all-gather.2.cloned.1.call-done = bf16[1024,4096]{1,0:T(8,128)(2,1)} async-done(((bf16[128,4096]{1,0:T(8,128)(2,1)}), bf16[1024,4096]{1,0:T(8,128)(2,1)}) %all-gather.2.cloned.1.call-update) | async-done | bytes 8388624 | tf_op jit(solution)/shard_map/all_gather | solution.py:55
  122.2 0.0 copy-done.6
  122.2 8.5 %fusion.5 = bf16[1024,1,512]{2,0,1:T(8,128)(2,1)S(1)} fusion(bf16[1024,4096]{1,0:T(8,128)(2,1)} %all-gather.2.cloned.1.call-done, bf16[1,4096,256]{2,1,0:T(8,128)(2,1)S(1)} %copy-done.6, bf16[1,4096,256]{2,1,0:T(8,128)(2,1)} %param.16), kind=kOutput, calls=%fused_computation.14 | convolution fusion | flops 4303880192 | bytes 13631488 | tf_op jit(solution)/shard_map/rd,ldc->rlc/dot_general | solution.py:53
  130.7 0.0 copy-done
  130.7 0.0 copy-done.7
  130.7 0.5 fusion.16
  131.2 0.4 fusion.3
  131.6 0.5 fusion.6
  132.1 0.8 copy.12
  (2 shorter events, 0.0 us)
Async XLA Ops:
  6.5 124.2 %copy-start = (bf16[1,512,256]{2,1,0:T(8,128)(2,1)S(1)}, bf16[1,512,256]{2,1,0:T(8,128)(2,1)}, u32[]{:S(2)}) copy-start(bf16[1,512,256]{2,1,0:T(8,128)(2,1)} %param.18) | copy-start | bytes 786436
  6.5 3.7 %copy-start.4 = (s32[64]{0:T(128)S(1)}, s32[64]{0:T(128)}, u32[]{:S(2)}) copy-start(s32[64]{0:T(128)} %param.13) | copy-start | bytes 772
  6.5 3.7 %copy-start.5 = (s32[64]{0:T(128)S(1)}, s32[64]{0:T(128)}, u32[]{:S(2)}) copy-start(s32[64]{0:T(128)} %param.12) | copy-start | bytes 772
  6.5 58.3 %copy-start.1 = (bf16[128,4096]{1,0:T(8,128)(2,1)S(1)}, bf16[128,4096]{1,0:T(8,128)(2,1)}, u32[]{:S(2)}) copy-start(bf16[128,4096]{1,0:T(8,128)(2,1)} %param.10) | copy-start | bytes 3145732
  6.5 58.3 %all-reduce.2.cloned.1.call-start = ((), (), s32[]{:S(2)}) async-start(), calls=%async_computation | async-start | bytes 2097152 | tf_op jit(solution)/shard_map/psum | solution.py:45
  10.1 56.5 %copy-start.3 = (f32[4096]{0:T(1024)S(1)}, f32[4096]{0:T(1024)}, u32[]{:S(2)}) copy-start(f32[4096]{0:T(1024)} %param.15) | copy-start | bytes 49156
  10.1 112.1 %all-gather.2.cloned.1.call-start = ((), (), s32[]{:S(2)}) async-start(), calls=%async_computation.1 | async-start | bytes 9437184 | tf_op jit(solution)/shard_map/all_gather | solution.py:55
  64.8 1.8 %copy-start.2 = (bf16[128,4096]{1,0:T(8,128)(2,1)S(1)}, bf16[128,4096]{1,0:T(8,128)(2,1)}, u32[]{:S(2)}) copy-start(bf16[128,4096]{1,0:T(8,128)(2,1)} %all-reduce.2.cloned.1.call-done) | copy-start | bytes 3145732
  66.7 55.6 %copy-start.6 = (bf16[1,4096,256]{2,1,0:T(8,128)(2,1)S(1)}, bf16[1,4096,256]{2,1,0:T(8,128)(2,1)}, u32[]{:S(2)}) copy-start(bf16[1,4096,256]{2,1,0:T(8,128)(2,1)} %param.17) | copy-start | bytes 6291460
  68.3 62.4 %copy-start.7 = (s32[512]{0:T(512)S(1)}, s32[512]{0:T(512)}, u32[]{:S(2)}) copy-start(s32[512]{0:T(512)} %param.19) | copy-start | bytes 6148
Sparse Core Ops, SparseCore 0:
  10.3 54.5 all-reduce.1
  68.4 53.7 all-gather.1
where the time goes:
time: 140 us
  waiting for transfers between devices  108 us (77%)
  between operations  13.5 us (10%)
  matrix products  10.5 us (8%)
  other arithmetic  6.41 us (5%)
    psum x1, waiting for transfers between devices, per_device(): summed = lax.psum(term.astype(jnp.bfloat16), 'layer').astype(jnp.float32)  54.5 us
    all_gather x1, waiting for transfers between devices, per_device(): lax.all_gather(normed, 'seq', axis=0, tiled=True)  53.9 us
    dot_general x1, matrix products, per_device(): jnp.einsum('rd,ldc->rlc', lax.all_gather(normed, 'seq', axis=0, tiled=Tru...  8.49 us
  transfers between devices with their start and end apart: 2, of which 2 were waited for; matrix products, arithmetic and copies ran while one was open for 0% of the time, Pallas kernels for 0%

commit v1 on v0

v1 whole, which is shorter than its diff:
```python
import functools

import jax
import jax.numpy as jnp
from jax import lax
from jax.experimental import pallas as pl
from jax.experimental.pallas import tpu as pltpu
from jax.sharding import PartitionSpec as P

MESH = pl.DeviceIdType.MESH
CH = 16
QBLK = 128


def kernel(
    S,
    L,
    start_ref,
    end_ref,
    which_ref,
    gain_ref,
    klen_ref,
    target_ref,
    source_ref,
    wk_ref,
    wv_ref,
    q_ref,
    out_ref,
    tgt,
    src,
    merged,
    owner,
    na,
    w,
    q,
    kv,
    scores,
    klen,
    local_sem,
    zs,
    zr,
    rs,
    rr,
    bs,
    br,
):
    rows, D = target_ref.shape
    C = rows // CH
    n = S // 2
    H = n // 2
    T = S * rows
    GR = S * CH
    spans = start_ref.shape[0]
    seglen = T // spans
    here = rows // seglen
    nq = q.shape[0]
    hd = q.shape[1]

    s = lax.axis_index("seq")
    z = lax.axis_index("layer")
    chip = s // 2
    core = s % 2
    sib = chip * 2 + (1 - core)

    def swap(p):
        up = (2 * p) // n
        return p * (1 - up) + up * (3 * n // 2 - 1 - p)

    pos = swap(chip)

    def seq_of(p):
        return swap((p + 2 * n) % n) * 2 + core

    nbr = (seq_of(pos + 1), seq_of(pos - 1))

    local = [
        pltpu.make_async_copy(source_ref.at[0], src, local_sem.at[0]),
        pltpu.make_async_copy(target_ref, tgt, local_sem.at[1]),
        pltpu.make_async_copy(wk_ref.at[0], w.at[0], local_sem.at[2]),
        pltpu.make_async_copy(wv_ref.at[0], w.at[1], local_sem.at[3]),
        pltpu.make_async_copy(q_ref.at[0], q, local_sem.at[4]),
    ]
    for copy in local:
        copy.start()

    barrier = pltpu.get_barrier_semaphore()
    for other in (
        {"seq": nbr[0]},
        {"seq": nbr[1]},
        {"seq": sib},
        {"layer": (z + 1) % L},
        {"layer": (z + L - 1) % L},
    ):
        pl.semaphore_signal(barrier, inc=1, device_id=other, device_id_type=MESH)
    pl.semaphore_wait(barrier, 5)

    def at_rows(c):
        return pl.ds(pl.multiple_of(c * CH, CH), CH)

    def z_copy(d, c, from_input=False):
        source = source_ref.at[0, at_rows(c)] if from_input else merged.at[d, at_rows(c)]
        return pltpu.make_async_remote_copy(
            src_ref=source,
            dst_ref=merged.at[d, at_rows(c)],
            send_sem=zs.at[d, c],
            recv_sem=zr.at[d, c],
            device_id={"layer": (z + 1 - 2 * d + L) % L},
            device_id_type=MESH,
        )

    def ring_copy(d, hop, c):
        origin = seq_of(pos + (-hop if d == 0 else hop))
        return pltpu.make_async_remote_copy(
            src_ref=na.at[origin, at_rows(c)],
            dst_ref=na.at[origin, at_rows(c)],
            send_sem=rs.at[d, hop, c],
            recv_sem=rr.at[d, hop, c],
            device_id={"seq": nbr[d]},
            device_id_type=MESH,
        )

    def sib_copy(rel, c):
        origin = seq_of(pos - rel)
        return pltpu.make_async_remote_copy(
            src_ref=na.at[origin, at_rows(c)],
            dst_ref=na.at[origin, at_rows(c)],
            send_sem=bs.at[rel, c],
            recv_sem=br.at[rel, c],
            device_id={"seq": sib},
            device_id_type=MESH,
        )

    @pl.when(z == 0)
    def _():
        @pl.loop(0, C)
        def _(c):
            z_copy(0, c, True).start()

    @pl.when(z == L - 1)
    def _():
        @pl.loop(0, C)
        def _(c):
            z_copy(1, c, True).start()

    row = s * rows + lax.broadcasted_iota(jnp.int32, (rows, 128), 0)
    own = jnp.full((rows, 128), -1, jnp.int32)
    for k in range(here):
        at = s * here + k
        inside = (row >= start_ref[at]) & (row < end_ref[at])
        own = jnp.where(inside, which_ref[at], own)
    owner[...] = own
    klen[...] = jnp.broadcast_to(klen_ref[...], (128, nq)).T

    local[0].wait()
    local[1].wait()

    def ownership(c):
        return jnp.broadcast_to(owner[at_rows(c), :1], (CH, D))

    def chain(d, c):
        behind = z * (1 - d) + d * (L - 1 - z)
        ahead = z * d + (1 - d) * (L - 1 - z)

        @pl.when(behind > 0)
        def _():
            z_copy(d, c).wait_recv()

            @pl.when(ahead > 0)
            def _():
                mine = src[at_rows(c), :].astype(jnp.float32)
                other = merged[d, at_rows(c), :].astype(jnp.float32)
                merged[d, at_rows(c), :] = jnp.where(ownership(c) == z, mine, other).astype(jnp.bfloat16)
                z_copy(d, c).start()

    first = (2 * z) // L

    def normalize(c):
        who = ownership(c)
        before = merged[0, at_rows(c), :].astype(jnp.float32)
        after = merged[1, at_rows(c), :].astype(jnp.float32)
        states = jnp.where(who < z, before, after)
        states = jnp.where(who == z, src[at_rows(c), :].astype(jnp.float32), states)
        states = jnp.where(who < 0, tgt[at_rows(c), :].astype(jnp.float32), states)
        meansq = jnp.mean(states * states, axis=-1, keepdims=True)
        na[s, at_rows(c), :] = (states * lax.rsqrt(meansq + 1e-06) * gain_ref[...]).astype(jnp.bfloat16)

    def project(c):
        x = na[:, at_rows(c), :].reshape(GR, D)
        keys = jnp.dot(x, w[0], preferred_element_type=jnp.float32).astype(jnp.bfloat16)
        values = jnp.dot(x, w[1], preferred_element_type=jnp.float32).astype(jnp.bfloat16)
        kv[pl.ds(pl.multiple_of(c * GR, GR), GR), :] = values
        scores[:, pl.ds(pl.multiple_of(c * GR, GR), GR)] = lax.dot_general(
            q[...], keys, (((1,), (1,)), ((), ())), preferred_element_type=jnp.float32
        )

    chain(first, 0)

    @pl.loop(0, C + H + 1)
    def _(i):
        @pl.when(i + 1 < C)
        def _():
            chain(first, i + 1)

        @pl.when(i < C)
        def _():
            chain(1 - first, i)
            normalize(i)
            ring_copy(0, 0, i).start()
            ring_copy(1, 0, i).start()
            sib_copy(0, i).start()

        for h in range(1, H + 1):
            c = i - h

            @pl.when((c >= 0) & (c < C))
            def _():
                for d in (0, 1):

                    def arrived(d=d):
                        ring_copy(d, h - 1, c).wait_recv()
                        if h + 1 < H:
                            ring_copy(d, h, c).start()
                        elif h + 1 == H:

                            @pl.when(c % 2 == d)
                            def _():
                                ring_copy(d, h, c).start()

                        sib_copy(h if d == 0 else n - h, c).start()

                    if h < H:
                        arrived()
                    else:
                        pl.when(c % 2 == d)(arrived)

        c = i - H - 1

        @pl.when(c >= 0)
        def _():
            @pl.when(c == 0)
            def _():
                for copy in local[2:]:
                    copy.wait()

            for rel in range(n):
                sib_copy(rel, c).wait_recv()
            project(c)

    col = lax.broadcasted_iota(jnp.int32, (QBLK, T), 1)
    token = (col % GR) // CH * rows + col // GR * CH + col % CH

    @pl.loop(0, nq // QBLK)
    def _(b):
        at = pl.ds(pl.multiple_of(b * QBLK, QBLK), QBLK)
        seen = token < jnp.broadcast_to(klen[at, :1], (QBLK, T))
        sc = jnp.where(seen, scores[at, :], -1e30)
        expo = jnp.exp(sc - jnp.max(sc, axis=-1, keepdims=True))
        probs = (expo * (1.0 / jnp.sum(expo, axis=-1, keepdims=True))).astype(jnp.bfloat16)
        out_ref[0, at, :] = jnp.dot(probs, kv[...], preferred_element_type=jnp.float32).astype(jnp.bfloat16)

    @pl.loop(0, C)
    def _(c):
        @pl.when(z < L - 1)
        def _():
            z_copy(0, c).wait_send()

        @pl.when(z > 0)
        def _():
            z_copy(1, c).wait_send()

        for d in (0, 1):
            for hop in range(H - 1):
                ring_copy(d, hop, c).wait_send()

            @pl.when(c % 2 == d)
            def _():
                ring_copy(d, H - 1, c).wait_send()

        for rel in range(n):
            sib_copy(rel, c).wait_send()


def per_device(
    S,
    L,
    target_enc,
    source_enc,
    span_start,
    span_end,
    span_source,
    norm_gain,
    w_key,
    w_value,
    queries,
    key_len,
):
    rows, D = target_enc.shape
    width = w_key.shape[2]
    nq = queries.shape[1]
    T = S * rows
    C = rows // CH
    n = S // 2
    smem = pl.BlockSpec(memory_space=pltpu.SMEM)
    vmem = pl.BlockSpec(memory_space=pltpu.VMEM)
    anywhere = pl.BlockSpec(memory_space=pl.ANY)
    bf16 = jnp.bfloat16
    return pl.pallas_call(
        functools.partial(kernel, S, L),
        out_shape=jax.ShapeDtypeStruct((1, nq, width), bf16),
        in_specs=[smem, smem, smem, vmem, vmem, anywhere, anywhere, anywhere, anywhere, anywhere],
        out_specs=vmem,
        scratch_shapes=[
            pltpu.VMEM((rows, D), bf16),
            pltpu.VMEM((rows, D), bf16),
            pltpu.VMEM((2, rows, D), bf16),
            pltpu.VMEM((rows, 128), jnp.int32),
            pltpu.VMEM((S, rows, D), bf16),
            pltpu.VMEM((2, D, width), bf16),
            pltpu.VMEM((nq, width), bf16),
            pltpu.VMEM((T, width), bf16),
            pltpu.VMEM((nq, T), jnp.float32),
            pltpu.VMEM((nq, 128), jnp.int32),
            pltpu.SemaphoreType.DMA((5,)),
            pltpu.SemaphoreType.DMA((2, C)),
            pltpu.SemaphoreType.DMA((2, C)),
            pltpu.SemaphoreType.DMA((2, n // 2, C)),
            pltpu.SemaphoreType.DMA((2, n // 2, C)),
            pltpu.SemaphoreType.DMA((n, C)),
            pltpu.SemaphoreType.DMA((n, C)),
        ],
        compiler_params=pltpu.CompilerParams(
            collective_id=0, has_side_effects=True, vmem_limit_bytes=56 << 20
        ),
    )(
        span_start,
        span_end,
        span_source,
        norm_gain.reshape(1, D),
        key_len.reshape(1, nq),
        target_enc,
        source_enc,
        w_key,
        w_value,
        queries,
    )


def solution(mesh):
    return jax.shard_map(
        functools.partial(per_device, mesh.shape["seq"], mesh.shape["layer"]),
        mesh=mesh,
        in_specs=(
            P("seq", None),
            P("layer", "seq", None),
            P(),
            P(),
            P(),
            P(),
            P("layer", None, "seq"),
            P("layer", None, "seq"),
            P("layer", None, "seq"),
            P(),
        ),
        out_specs=P("layer", None, "seq"),
        check_vma=False,
    )
```

time: 140 us -> 68.6 us (0.49)
  waiting for transfers between devices: 108 us -> 0 us
  Pallas kernels: 0 us -> 66.7 us
  between operations: 13.5 us -> 0.01 us
  matrix products: 10.5 us -> 0 us
  other arithmetic: 6.41 us -> 0 us
    pallas_call x0 -> x1, Pallas kernels: none -> 66.7 us  [per_device(): pl.pallas_call(functools.partial(kernel, S, L), out_shape=jax.ShapeDtypeS...]
    psum x1 -> x0, waiting for transfers between devices: 54.5 us -> none  [per_device(): summed = lax.psum(term.astype(jnp.bfloat16), 'layer').astype(jnp.float32)]
    all_gather x1 -> x0, waiting for transfers between devices: 53.9 us -> none  [per_device(): lax.all_gather(normed, 'seq', axis=0, tiled=True)]
    dot_general x4 -> x0, matrix products: 10.5 us -> none  [the longest x1 8.49 us: per_device(): jnp.einsum('rd,ldc->rlc', lax.all_gather(normed, 'seq', axis=0, tiled=Tru...]
    convert_element_type x2 -> x0, other arithmetic: 4.12 us -> none  [the longest x1 2.53 us: per_device(): summed = lax.psum(term.astype(jnp.bfloat16), 'layer').astype(jnp.float32)]
    reduce_sum x2 -> x0, other arithmetic: 2.17 us -> none  [the longest x1 1.81 us: per_device(): meansq = jnp.mean(states * states, axis=-1, keepdims=True)]
    unnamed x16 -> x1, local copies, waits for them, and re-layouts: 0.04 us -> 1.67 us
  transfers between devices with their start and end apart: 2 -> 0, of which waited for: 2 -> 0; matrix products, arithmetic and copies ran while one was open for 0% -> 0% of each run, Pallas kernels for 0% -> 0%
where the time goes in v1:
time: 68.6 us; the launch traced here: 68.4 us
  Pallas kernels  66.7 us (97%)
  local copies, waits for them, and re-layouts  1.67 us (2%)
    pallas_call x1, Pallas kernels, per_device(): pl.pallas_call(functools.partial(kernel, S, L), out_shape=jax.ShapeDtypeS...  66.7 us
    unnamed x1, local copies, waits for them, and re-layouts  1.67 us

profile of v1, /device:TPU:0, one launch (start us, length us, event | category | flops | bytes accessed | tf_op | source)
XLA Modules:
  0.0 68.4 jit_solution(6366886724640275963)
XLA Ops:
  0.0 66.7 %shard_map.100 = bf16[1,512,256]{2,1,0:T(8,128)(2,1)} custom-call(s32[64]{0:T(128)} %start_ref.1, s32[64]{0:T(128)} %end_ref.1, s32[64]{0:T(128)} %which_ref.1, f32[1,4096]{1,0:T(1,128)} %bitcast.2, s32[1,512]{1,0:T(1,128)} %bitcast.3, bf16[128,4096]{1,0:T(8,128)(2,1)} %target_ref.1, bf16[1,128,4096]{2,1,0:T(8,128)(2,1)} %source_ref.1, ...), custom_call_target="tpu_custom_call" | custom-call | tf_op jit(solution)/shard_map/pallas_call | solution.py:307
  66.7 1.7 %copy.12 = bf16[1,512,256]{2,1,0:T(8,128)(2,1)} copy(bf16[1,512,256]{2,1,0:T(8,128)(2,1)} %shard_map.100) | data formatting | bytes 524288

commit v2 on v1

--- a/solution.py
+++ b/solution.py
@@ -9,6 +9,8 @@
 
 MESH = pl.DeviceIdType.MESH
 CH = 16
+PIECES = 2
+AHEAD = 3
 QBLK = 128
 
 
@@ -97,22 +99,24 @@
     def at_rows(c):
         return pl.ds(pl.multiple_of(c * CH, CH), CH)
 
-    def z_copy(d, c, from_input=False):
-        source = source_ref.at[0, at_rows(c)] if from_input else merged.at[d, at_rows(c)]
+    def z_copy(d, c, p, from_input=False):
+        cols = pl.ds(p * (D // PIECES), D // PIECES)
+        source = source_ref.at[0, at_rows(c), cols] if from_input else merged.at[d, at_rows(c), cols]
         return pltpu.make_async_remote_copy(
             src_ref=source,
-            dst_ref=merged.at[d, at_rows(c)],
-            send_sem=zs.at[d, c],
-            recv_sem=zr.at[d, c],
+            dst_ref=merged.at[d, at_rows(c), cols],
+            send_sem=zs.at[d, c, p],
+            recv_sem=zr.at[d, c, p],
             device_id={"layer": (z + 1 - 2 * d + L) % L},
             device_id_type=MESH,
         )
 
     def ring_copy(d, hop, c):
         origin = seq_of(pos + (-hop if d == 0 else hop))
+        cols = pl.ds(d * (D // 2), D // 2) if hop == H - 1 else pl.ds(0, D)
         return pltpu.make_async_remote_copy(
-            src_ref=na.at[origin, at_rows(c)],
-            dst_ref=na.at[origin, at_rows(c)],
+            src_ref=na.at[origin, at_rows(c), cols],
+            dst_ref=na.at[origin, at_rows(c), cols],
             send_sem=rs.at[d, hop, c],
             recv_sem=rr.at[d, hop, c],
             device_id={"seq": nbr[d]},
@@ -120,10 +124,11 @@
         )
 
     def sib_copy(rel, c):
-        origin = seq_of(pos - rel)
+        origin = seq_of(pos - (H if rel == n else rel))
+        cols = pl.ds((rel // n) * (D // 2), D // 2) if rel in (H, n) else pl.ds(0, D)
         return pltpu.make_async_remote_copy(
-            src_ref=na.at[origin, at_rows(c)],
-            dst_ref=na.at[origin, at_rows(c)],
+            src_ref=na.at[origin, at_rows(c), cols],
+            dst_ref=na.at[origin, at_rows(c), cols],
             send_sem=bs.at[rel, c],
             recv_sem=br.at[rel, c],
             device_id={"seq": sib},
@@ -134,13 +139,15 @@
     def _():
         @pl.loop(0, C)
         def _(c):
-            z_copy(0, c, True).start()
+            for p in range(PIECES):
+                z_copy(0, c, p, True).start()
 
     @pl.when(z == L - 1)
     def _():
         @pl.loop(0, C)
         def _(c):
-            z_copy(1, c, True).start()
+            for p in range(PIECES):
+                z_copy(1, c, p, True).start()
 
     row = s * rows + lax.broadcasted_iota(jnp.int32, (rows, 128), 0)
     own = jnp.full((rows, 128), -1, jnp.int32)
@@ -161,16 +168,21 @@
         behind = z * (1 - d) + d * (L - 1 - z)
         ahead = z * d + (1 - d) * (L - 1 - z)
 
-        @pl.when(behind > 0)
-        def _():
-            z_copy(d, c).wait_recv()
-
-            @pl.when(ahead > 0)
-            def _():
-                mine = src[at_rows(c), :].astype(jnp.float32)
-                other = merged[d, at_rows(c), :].astype(jnp.float32)
-                merged[d, at_rows(c), :] = jnp.where(ownership(c) == z, mine, other).astype(jnp.bfloat16)
-                z_copy(d, c).start()
+        @pl.when((behind > 0) & (ahead > 0))
+        def _():
+            who = jnp.broadcast_to(owner[at_rows(c), :1], (CH, D // PIECES))
+            for p in range(PIECES):
+                cols = pl.ds(p * (D // PIECES), D // PIECES)
+                z_copy(d, c, p).wait_recv()
+                mine = src[at_rows(c), cols].astype(jnp.float32)
+                other = merged[d, at_rows(c), cols].astype(jnp.float32)
+                merged[d, at_rows(c), cols] = jnp.where(who == z, mine, other).astype(jnp.bfloat16)
+                z_copy(d, c, p).start()
+
+        @pl.when((behind > 0) & (ahead == 0))
+        def _():
+            for p in range(PIECES):
+                z_copy(d, c, p).wait_recv()
 
     first = (2 * z) // L
 
@@ -193,17 +205,31 @@
             q[...], keys, (((1,), (1,)), ((), ())), preferred_element_type=jnp.float32
         )
 
-    chain(first, 0)
+    middle = (z > 0) & (z < L - 1)
+
+    @pl.when(middle)
+    def _():
+        for k in range(min(AHEAD, C)):
+            chain(first, k)
+            if k > 0:
+                chain(1 - first, k - 1)
 
     @pl.loop(0, C + H + 1)
     def _(i):
-        @pl.when(i + 1 < C)
-        def _():
-            chain(first, i + 1)
+        @pl.when(middle & (i + AHEAD < C))
+        def _():
+            chain(first, i + AHEAD)
+
+        @pl.when(middle & (i + AHEAD - 1 < C))
+        def _():
+            chain(1 - first, i + AHEAD - 1)
 
         @pl.when(i < C)
         def _():
-            chain(1 - first, i)
+            @pl.when(jnp.logical_not(middle))
+            def _():
+                chain(1 - first, i)
+
             normalize(i)
             ring_copy(0, 0, i).start()
             ring_copy(1, 0, i).start()
@@ -215,23 +241,11 @@
             @pl.when((c >= 0) & (c < C))
             def _():
                 for d in (0, 1):
-
-                    def arrived(d=d):
-                        ring_copy(d, h - 1, c).wait_recv()
-                        if h + 1 < H:
-                            ring_copy(d, h, c).start()
-                        elif h + 1 == H:
-
-                            @pl.when(c % 2 == d)
-                            def _():
-                                ring_copy(d, h, c).start()
-
-                        sib_copy(h if d == 0 else n - h, c).start()
-
+                    ring_copy(d, h - 1, c).wait_recv()
                     if h < H:
-                        arrived()
-                    else:
-                        pl.when(c % 2 == d)(arrived)
+                        ring_copy(d, h, c).start()
+                for d in (0, 1):
+                    sib_copy(h if d == 0 else (n if h == H else n - h), c).start()
 
         c = i - H - 1
 
@@ -242,7 +256,7 @@
                 for copy in local[2:]:
                     copy.wait()
 
-            for rel in range(n):
+            for rel in range(n + 1):
                 sib_copy(rel, c).wait_recv()
             project(c)
 
@@ -262,21 +276,19 @@
     def _(c):
         @pl.when(z < L - 1)
         def _():
-            z_copy(0, c).wait_send()
+            for p in range(PIECES):
+                z_copy(0, c, p).wait_send()
 
         @pl.when(z > 0)
         def _():
-            z_copy(1, c).wait_send()
+            for p in range(PIECES):
+                z_copy(1, c, p).wait_send()
 
         for d in (0, 1):
-            for hop in range(H - 1):
+            for hop in range(H):
                 ring_copy(d, hop, c).wait_send()
 
-            @pl.when(c % 2 == d)
-            def _():
-                ring_copy(d, H - 1, c).wait_send()
-
-        for rel in range(n):
+        for rel in range(n + 1):
             sib_copy(rel, c).wait_send()
 
 
@@ -321,12 +333,12 @@
             pltpu.VMEM((nq, T), jnp.float32),
             pltpu.VMEM((nq, 128), jnp.int32),
             pltpu.SemaphoreType.DMA((5,)),
-            pltpu.SemaphoreType.DMA((2, C)),
-            pltpu.SemaphoreType.DMA((2, C)),
+            pltpu.SemaphoreType.DMA((2, C, PIECES)),
+            pltpu.SemaphoreType.DMA((2, C, PIECES)),
             pltpu.SemaphoreType.DMA((2, n // 2, C)),
             pltpu.SemaphoreType.DMA((2, n // 2, C)),
-            pltpu.SemaphoreType.DMA((n, C)),
-            pltpu.SemaphoreType.DMA((n, C)),
+            pltpu.SemaphoreType.DMA((n + 1, C)),
+            pltpu.SemaphoreType.DMA((n + 1, C)),
         ],
         compiler_params=pltpu.CompilerParams(
             collective_id=0, has_side_effects=True, vmem_limit_bytes=56 << 20

time: 68.6 us -> 65.4 us (0.953)
  Pallas kernels: 66.7 us -> 63.5 us
    pallas_call x1, Pallas kernels: 66.7 us -> 63.5 us  [per_device(): pl.pallas_call(functools.partial(kernel, S, L), out_shape=jax.ShapeDtypeS...]
where the time goes in v2:
time: 65.4 us; the launch traced here: 65.2 us
  Pallas kernels  63.5 us (97%)
  local copies, waits for them, and re-layouts  1.67 us (3%)
    pallas_call x1, Pallas kernels, per_device(): pl.pallas_call(functools.partial(kernel, S, L), out_shape=jax.ShapeDtypeS...  63.5 us
    unnamed x1, local copies, waits for them, and re-layouts  1.67 us

profile of v2, /device:TPU:0, one launch (start us, length us, event | category | flops | bytes accessed | tf_op | source)
XLA Modules:
  0.0 65.2 jit_solution(10295370608873170839)
XLA Ops:
  0.0 63.5 %shard_map.100 = bf16[1,512,256]{2,1,0:T(8,128)(2,1)} custom-call(s32[64]{0:T(128)} %start_ref.1, s32[64]{0:T(128)} %end_ref.1, s32[64]{0:T(128)} %which_ref.1, f32[1,4096]{1,0:T(1,128)} %bitcast.2, s32[1,512]{1,0:T(1,128)} %bitcast.3, bf16[128,4096]{1,0:T(8,128)(2,1)} %target_ref.1, bf16[1,128,4096]{2,1,0:T(8,128)(2,1)} %source_ref.1, ...), custom_call_target="tpu_custom_call" | custom-call | tf_op jit(solution)/shard_map/pallas_call | solution.py:319
  63.5 1.7 %copy.12 = bf16[1,512,256]{2,1,0:T(8,128)(2,1)} copy(bf16[1,512,256]{2,1,0:T(8,128)(2,1)} %shard_map.100) | data formatting | bytes 524288

commit v3 on v2

--- a/solution.py
+++ b/solution.py
@@ -10,8 +10,9 @@
 MESH = pl.DeviceIdType.MESH
 CH = 16
 PIECES = 2
-AHEAD = 3
-QBLK = 128
+AHEAD = 2
+SKEW = 3
+QBLK = 512
 
 
 def kernel(
@@ -97,16 +98,18 @@
     pl.semaphore_wait(barrier, 5)
 
     def at_rows(c):
+        if c is None:
+            return pl.ds(0, rows)
         return pl.ds(pl.multiple_of(c * CH, CH), CH)
 
     def z_copy(d, c, p, from_input=False):
-        cols = pl.ds(p * (D // PIECES), D // PIECES)
+        cols = pl.ds(0, D) if p is None else pl.ds(p * (D // PIECES), D // PIECES)
         source = source_ref.at[0, at_rows(c), cols] if from_input else merged.at[d, at_rows(c), cols]
         return pltpu.make_async_remote_copy(
             src_ref=source,
             dst_ref=merged.at[d, at_rows(c), cols],
-            send_sem=zs.at[d, c, p],
-            recv_sem=zr.at[d, c, p],
+            send_sem=zs.at[d],
+            recv_sem=zr.at[d, 0 if c is None else c, 0 if p is None else p],
             device_id={"layer": (z + 1 - 2 * d + L) % L},
             device_id_type=MESH,
         )
@@ -117,8 +120,8 @@
         return pltpu.make_async_remote_copy(
             src_ref=na.at[origin, at_rows(c), cols],
             dst_ref=na.at[origin, at_rows(c), cols],
-            send_sem=rs.at[d, hop, c],
-            recv_sem=rr.at[d, hop, c],
+            send_sem=rs.at[d, hop],
+            recv_sem=rr.at[d, hop, 0 if c is None else c],
             device_id={"seq": nbr[d]},
             device_id_type=MESH,
         )
@@ -129,8 +132,8 @@
         return pltpu.make_async_remote_copy(
             src_ref=na.at[origin, at_rows(c), cols],
             dst_ref=na.at[origin, at_rows(c), cols],
-            send_sem=bs.at[rel, c],
-            recv_sem=br.at[rel, c],
+            send_sem=bs.at[rel],
+            recv_sem=br.at[rel, 0 if c is None else c],
             device_id={"seq": sib},
             device_id_type=MESH,
         )
@@ -214,7 +217,7 @@
             if k > 0:
                 chain(1 - first, k - 1)
 
-    @pl.loop(0, C + H + 1)
+    @pl.loop(0, C + SKEW * H + 1)
     def _(i):
         @pl.when(middle & (i + AHEAD < C))
         def _():
@@ -236,7 +239,7 @@
             sib_copy(0, i).start()
 
         for h in range(1, H + 1):
-            c = i - h
+            c = i - SKEW * h
 
             @pl.when((c >= 0) & (c < C))
             def _():
@@ -247,7 +250,7 @@
                 for d in (0, 1):
                     sib_copy(h if d == 0 else (n if h == H else n - h), c).start()
 
-        c = i - H - 1
+        c = i - SKEW * H - 1
 
         @pl.when(c >= 0)
         def _():
@@ -272,24 +275,20 @@
         probs = (expo * (1.0 / jnp.sum(expo, axis=-1, keepdims=True))).astype(jnp.bfloat16)
         out_ref[0, at, :] = jnp.dot(probs, kv[...], preferred_element_type=jnp.float32).astype(jnp.bfloat16)
 
-    @pl.loop(0, C)
-    def _(c):
-        @pl.when(z < L - 1)
-        def _():
-            for p in range(PIECES):
-                z_copy(0, c, p).wait_send()
-
-        @pl.when(z > 0)
-        def _():
-            for p in range(PIECES):
-                z_copy(1, c, p).wait_send()
-
-        for d in (0, 1):
-            for hop in range(H):
-                ring_copy(d, hop, c).wait_send()
-
-        for rel in range(n + 1):
-            sib_copy(rel, c).wait_send()
+    @pl.when(z < L - 1)
+    def _():
+        z_copy(0, None, None).wait_send()
+
+    @pl.when(z > 0)
+    def _():
+        z_copy(1, None, None).wait_send()
+
+    for d in (0, 1):
+        for hop in range(H):
+            ring_copy(d, hop, None).wait_send()
+
+    for rel in range(n + 1):
+        sib_copy(rel, None).wait_send()
 
 
 def per_device(
@@ -333,11 +332,11 @@
             pltpu.VMEM((nq, T), jnp.float32),
             pltpu.VMEM((nq, 128), jnp.int32),
             pltpu.SemaphoreType.DMA((5,)),
+            pltpu.SemaphoreType.DMA((2,)),
             pltpu.SemaphoreType.DMA((2, C, PIECES)),
-            pltpu.SemaphoreType.DMA((2, C, PIECES)),
+            pltpu.SemaphoreType.DMA((2, n // 2)),
             pltpu.SemaphoreType.DMA((2, n // 2, C)),
-            pltpu.SemaphoreType.DMA((2, n // 2, C)),
-            pltpu.SemaphoreType.DMA((n + 1, C)),
+            pltpu.SemaphoreType.DMA((n + 1,)),
             pltpu.SemaphoreType.DMA((n + 1, C)),
         ],
         compiler_params=pltpu.CompilerParams(

time: 65.4 us -> 62.3 us (0.953)
  Pallas kernels: 63.5 us -> 60.4 us
    pallas_call x1, Pallas kernels: 63.5 us -> 60.4 us  [per_device(): pl.pallas_call(functools.partial(kernel, S, L), out_shape=jax.ShapeDtypeS...]
where the time goes in v3:
time: 62.3 us; the launch traced here: 62.1 us
  Pallas kernels  60.4 us (97%)
  local copies, waits for them, and re-layouts  1.67 us (3%)
    pallas_call x1, Pallas kernels, per_device(): pl.pallas_call(functools.partial(kernel, S, L), out_shape=jax.ShapeDtypeS...  60.4 us
    unnamed x1, local copies, waits for them, and re-layouts  1.67 us

profile of v3, /device:TPU:0, one launch (start us, length us, event | category | flops | bytes accessed | tf_op | source)
XLA Modules:
  0.0 62.1 jit_solution(155418838022811896)
XLA Ops:
  0.0 60.4 %shard_map.100 = bf16[1,512,256]{2,1,0:T(8,128)(2,1)} custom-call(s32[64]{0:T(128)} %start_ref.1, s32[64]{0:T(128)} %end_ref.1, s32[64]{0:T(128)} %which_ref.1, f32[1,4096]{1,0:T(1,128)} %bitcast.2, s32[1,512]{1,0:T(1,128)} %bitcast.3, bf16[128,4096]{1,0:T(8,128)(2,1)} %target_ref.1, bf16[1,128,4096]{2,1,0:T(8,128)(2,1)} %source_ref.1, ...), custom_call_target="tpu_custom_call" | custom-call | tf_op jit(solution)/shard_map/pallas_call | solution.py:318
  60.4 1.7 %copy.12 = bf16[1,512,256]{2,1,0:T(8,128)(2,1)} copy(bf16[1,512,256]{2,1,0:T(8,128)(2,1)} %shard_map.100) | data formatting | bytes 524288
